TPU v7x, 512 devices: a whole 4x8x8 slice. The times are simulated.
512 devices in a mesh: batch: 16 (over y, core), seq: 32 (over x, z).
Axes of the slice: x: 4, y: 8, z: 8, core: 2. Of those that a mesh axis runs over, the one named last changes fastest.
Arguments:
- tokens: bfloat16 [16, 16384, 768], P('batch', 'seq'), may hold values from -6 to 6
- slide_lengths: int32 [16], P('batch'), may hold values from 2048 to 16384, as said below
- conv_weight: float32 [5, 768], replicated, may hold values from -2.5 to 2.5
- norm_gain: float32 [768], replicated, may hold values from 0.1 to 1.9
- w_query: bfloat16 [768, 768], P('batch'), may hold values from -8 to 8
- w_keyvalue: bfloat16 [768, 1536], P('batch'), may hold values from -0.21875 to 0.21875
- w_out: bfloat16 [768, 768], P('batch'), may hold values from -0.625 to 0.625
Outputs:
- result: bfloat16 [16, 16384, 768], P('batch', 'seq')
Inputs may be any that keep to these rules, and one draw needn't show every extreme that they name: `slide_lengths`: some slide uses all 16384 token slots.
All inputs are finite; a program needn't handle non-finite values.
Results may differ from a plain program's by a relative error of at most 0.0055.
The roundings to bfloat16 on the way count: a program that leaves them out, or rounds other values in their place, can miss the bound.
Values may be sent and summed in bfloat16 or wider, within the bound.
A program may use at most 64 MiB of HBM per device.

v0:
```python
import math
import jax
import jax.numpy as jnp
from jax import lax
from jax.sharding import PartitionSpec as P

HEADS = 12
GROUP = 4
CONV_TAP_COUNT = 5
CONV_DILATION = 3


def with_halo(cells, sides, width):
    for axis, dim in sides:
        count = lax.axis_size(axis)
        ends = count - 1
        head = lax.slice_in_dim(cells, 0, width, axis=dim)
        tail = lax.slice_in_dim(cells, cells.shape[dim] - width, cells.shape[dim], axis=dim)
        cells = jnp.concatenate(
            [
                lax.ppermute(tail, axis, [(i, (i + 1) % count) for i in range(ends)]),
                cells,
                lax.ppermute(head, axis, [((i + 1) % count, i) for i in range(ends)]),
            ],
            axis=dim,
        )
    return cells


def partner_2(block, axis, stride):
    count = lax.axis_size(axis)
    route = []
    for low in range(count):
        high = low | 1 << stride
        if high != low and high < count:
            route += [(low, high), (high, low)]
    return lax.ppermute(block, axis, route)


def start_state(batch_count, row_count, head_size):
    return (
        jnp.full((batch_count, row_count), -1e30, jnp.float32),
        jnp.zeros((batch_count, row_count), jnp.float32),
        jnp.zeros((batch_count, row_count, head_size), jnp.float32),
    )


def absorb(carry_state, query_vectors, key_vectors, value_vectors, usable, part_count):

    def split_parts(array):
        return array.reshape((part_count, array.shape[0] // part_count) + array.shape[1:])

    def update(item_tuple):
        (
            running_max,
            running_sum,
            weighted_values,
            query_segment_block,
            key_segment_block,
            value_block,
            usable_block,
        ) = item_tuple
        score_matrix = jnp.einsum(
            "ftl,fhl->fth",
            query_segment_block,
            key_segment_block,
            preferred_element_type=jnp.float32,
        )
        score_matrix = jnp.where(usable_block[:, None, :], score_matrix, -1000000000.0)
        new_max = jnp.maximum(running_max, jnp.max(score_matrix, axis=-1))
        exponent = jnp.exp(score_matrix - new_max[..., None])
        factor = jnp.exp(running_max - new_max)
        new_sum = running_sum * factor + jnp.sum(exponent, axis=-1)
        new_weighted = weighted_values * factor[..., None] + jnp.einsum(
            "hcp,hpu->hcu",
            exponent.astype(jnp.bfloat16),
            value_block,
            preferred_element_type=jnp.float32,
        )
        return (new_max, new_sum, new_weighted)

    pieces = tuple(
        (
            split_parts(array)
            for array in carry_state + (query_vectors, key_vectors, value_vectors, usable)
        )
    )
    updated = lax.map(update, pieces)
    return tuple((array.reshape((-1,) + array.shape[2:]) for array in updated))


def finish(carry_state):
    running_max, running_sum, weighted_values = carry_state
    return (weighted_values / running_sum[..., None], running_max + jnp.log(running_sum))


def pick_rows(array, rate, head_count):
    grouped = array.reshape(head_count, array.shape[1] // rate, rate, array.shape[2])
    return jnp.stack([grouped[head, :, head % rate, :] for head in range(head_count)])


def spread_rows(outputs, log_total, rate, head_count):
    chosen = jnp.arange(rate)[None, :] == (jnp.arange(head_count) % rate)[:, None]
    full_out = jnp.where(chosen[:, None, :, None], outputs[:, :, None, :], 0.0).reshape(
        head_count, -1, outputs.shape[2]
    )
    full_log = jnp.where(chosen[:, None, :], log_total[:, :, None], -jnp.inf).reshape(
        head_count, -1
    )
    return (full_out, full_log)


def on_device(tokens, slide_lengths, conv_weight, norm_gain, w_query, w_keyvalue, w_out):
    tok_rows = tokens.shape[1]
    model_width = tokens.shape[2]
    head_count = HEADS
    head_size = model_width // head_count
    seq_count = lax.axis_size("seq")
    seq_index = lax.axis_index("seq")
    first_row = seq_index * tok_rows
    length = slide_lengths[0]
    position = first_row + jnp.arange(tok_rows, dtype=jnp.int32)
    live_rows = position < length
    masked = jnp.where(live_rows[:, None], tokens[0], jnp.zeros_like(tokens[0]))
    border_padding = CONV_DILATION * (CONV_TAP_COUNT // 2)
    padded = with_halo(masked, (("seq", 0),), border_padding)
    mixed_rows = masked.astype(jnp.float32)
    for filter_tap_index in range(CONV_TAP_COUNT):
        tap_shift_amount = border_padding + (filter_tap_index - CONV_TAP_COUNT // 2) * CONV_DILATION
        mixed_rows = mixed_rows + conv_weight[filter_tap_index] * padded[
            tap_shift_amount : tap_shift_amount + tok_rows
        ].astype(jnp.float32)
    average = jnp.mean(mixed_rows, axis=-1, keepdims=True)
    centered = mixed_rows - average
    variance = jnp.mean(centered * centered, axis=-1, keepdims=True)
    normed = (centered * lax.rsqrt(variance + 1e-05) * norm_gain).astype(jnp.bfloat16)
    piece_rows = (
        lax.all_gather(w_query, "batch", axis=0, tiled=True),
        lax.all_gather(w_keyvalue, "batch", axis=0, tiled=True),
    )
    columns = normed
    query_sum = jnp.dot(columns, piece_rows[0], preferred_element_type=jnp.float32)
    pair_sum = jnp.dot(columns, piece_rows[1], preferred_element_type=jnp.float32)
    query_vectors = (query_sum * (1.0 / math.sqrt(head_size))).astype(jnp.bfloat16)
    key_value = pair_sum.astype(jnp.bfloat16)
    query_heads = query_vectors.reshape(tok_rows, head_count, head_size).transpose(1, 0, 2)
    key_heads = (
        key_value[:, :model_width].reshape(tok_rows, head_count, head_size).transpose(1, 0, 2)
    )
    value_heads = (
        key_value[:, model_width:].reshape(tok_rows, head_count, head_size).transpose(1, 0, 2)
    )
    head_index = jnp.arange(head_count, dtype=jnp.int32)
    dense_usable = jnp.broadcast_to(live_rows[None, :], (head_count, tok_rows))
    dense_state = absorb(
        start_state(head_count, tok_rows, head_size),
        query_heads,
        key_heads,
        value_heads,
        dense_usable,
        3,
    )
    dense_out, dense_log = finish(dense_state)
    group_rows = tok_rows // GROUP
    group_offsets = head_index % GROUP
    group_queries = pick_rows(query_heads, GROUP, head_count)
    group_block = jnp.stack(
        [pick_rows(key_heads, GROUP, head_count), pick_rows(value_heads, GROUP, head_count)]
    )
    for bit_number in range(GROUP.bit_length() - 1):
        partner = partner_2(group_block, "seq", bit_number)
        upper_half = seq_index >> bit_number & 1 == 1
        group_block = jnp.where(
            upper_half,
            jnp.concatenate([partner, group_block], axis=2),
            jnp.concatenate([group_block, partner], axis=2),
        )
    group_first = seq_index // GROUP * GROUP * tok_rows
    block_steps = GROUP * jnp.arange(GROUP * group_rows, dtype=jnp.int32)
    block_usable = group_first + block_steps[None, :] + group_offsets[:, None] < length
    group_state = absorb(
        start_state(head_count, group_rows, head_size),
        group_queries,
        group_block[0],
        group_block[1],
        block_usable,
        3,
    )
    group_out, group_log = finish(group_state)
    group_out, group_log = spread_rows(group_out, group_log, GROUP, head_count)
    slide_rows = tok_rows // seq_count
    slide_offsets = head_index % seq_count
    slide_queries_own = pick_rows(query_heads, seq_count, head_count)
    slide_keys_own = pick_rows(key_heads, seq_count, head_count)
    slide_values_own = pick_rows(value_heads, seq_count, head_count)
    slide_pairs = jnp.stack([slide_keys_own, slide_values_own])
    piece_rows = lax.all_gather(slide_pairs, "seq", axis=2, tiled=True)
    count = piece_rows.shape[2]
    key_positions = seq_count * jnp.arange(count, dtype=jnp.int32)[None, :] + slide_offsets[:, None]
    slide_state = absorb(
        start_state(head_count, slide_rows, head_size),
        slide_queries_own,
        piece_rows[0],
        piece_rows[1],
        key_positions < length,
        1,
    )
    slide_out, slide_log = finish(slide_state)
    slide_out, slide_log = spread_rows(slide_out, slide_log, seq_count, head_count)
    highest = jnp.maximum(jnp.maximum(dense_log, group_log), slide_log)
    dense_factor = jnp.exp(dense_log - highest)
    group_factor = jnp.exp(group_log - highest)
    slide_factor = jnp.exp(slide_log - highest)
    numer = (
        dense_factor[..., None] * dense_out
        + group_factor[..., None] * group_out
        + slide_factor[..., None] * slide_out
    )
    denom = dense_factor + group_factor + slide_factor
    combined = jnp.where(live_rows[None, :, None], numer / denom[..., None], 0.0)
    attention = combined.transpose(1, 0, 2).reshape(tok_rows, model_width).astype(jnp.bfloat16)
    columns = attention
    projected = jnp.dot(
        columns,
        lax.all_gather(w_out, "batch", axis=0, tiled=True),
        preferred_element_type=jnp.float32,
    )
    return projected.astype(jnp.bfloat16).reshape(1, tok_rows, model_width)


def solution(mesh):
    return jax.shard_map(
        on_device,
        mesh=mesh,
        in_specs=(
            P("batch", "seq", None),
            P("batch"),
            P(),
            P(),
            P("batch", None),
            P("batch", None),
            P("batch", None),
        ),
        out_specs=P("batch", "seq", None),
        check_vma=False,
    )
```

profile of v0, /device:TPU:1, one launch (start us, length us, event | category | flops | bytes accessed | tf_op | source)
XLA Modules:
  0.0 283.2 jit_solution(16786506327512890809)
XLA Ops:
  8.0 1.3 bitcast_select_fusion.1
  9.3 4.8 %collective-permute-start = (bf16[6,768]{1,0:T(8,128)(2,1)S(1)}, bf16[6,768]{1,0:T(8,128)(2,1)S(1)}, u32[]{:S(2)}, u32[]{:S(2)}) collective-permute-start(bf16[6,768]{1,0:T(8,128)(2,1)S(1)} %get-tuple-element.344), channel_id=1, source_target_pairs={{0,1},{1,2},{2,3},{3,4},{4,5},{5,6},{6,7},{7,8},{8,9},{9,10},{10,1... | collective-permute-start | bytes 27656 | tf_op jit(solution)/shard_map/ppermute | solution.py:21
  14.1 1.3 collective-permute-start.1
  15.6 3.6 %collective-permute-done.1 = bf16[6,768]{1,0:T(8,128)(2,1)S(1)} collective-permute-done((bf16[6,768]{1,0:T(8,128)(2,1)S(1)}, bf16[6,768]{1,0:T(8,128)(2,1)S(1)}, u32[]{:S(2)}, u32[]{:S(2)}) %collective-permute-start.1) | collective-permute-done | bytes 9248 | tf_op jit(solution)/shard_map/ppermute | solution.py:23
  20.7 37.1 %all-gather.7.cloned.1.call-done = bf16[768,1536]{1,0:T(8,128)(2,1)} async-done(((bf16[48,1536]{1,0:T(8,128)(2,1)}), bf16[768,1536]{1,0:T(8,128)(2,1)}) %all-gather.7.cloned.1.call-update) | async-done | bytes 2359312 | tf_op jit(solution)/shard_map/all_gather | solution.py:139
  57.8 3.1 %convolution_convert_fusion = bf16[512,1536]{1,0:T(8,128)(2,1)S(1)} fusion(bf16[768,1536]{1,0:T(8,128)(2,1)} %all-gather.7.cloned.1.call-done, f32[512,768]{1,0:T(8,128)S(1)} %get-tuple-element.253, f32[768]{0:T(1024)S(1)} %copy-done.15, f32[512]{0:T(512)S(1)} %add_rsqrt_fusion, f32[512]{0:T(512)S(1)} %broadcast_multiply_fusion), kind=kOutput, calls=%fused_computation.64 | convolution fusion | flops 1210318848 | bytes 5512192 | tf_op jit(solution)/shard_map/dot_general | solution.py:143
  62.2 1.5 copy.1435
  64.8 1.4 copy.1421
  66.2 1.6 copy.1448
  72.3 27.5 %all-gather.5.cloned.1.call-done = bf16[768,768]{1,0:T(8,128)(2,1)} async-done(((bf16[48,768]{1,0:T(8,128)(2,1)}), bf16[768,768]{1,0:T(8,128)(2,1)}) %all-gather.5.cloned.1.call-update) | async-done | bytes 1179664 | tf_op jit(solution)/shard_map/all_gather | solution.py:138
  99.9 3.0 %multiply_convert_fusion = bf16[512,768]{1,0:T(8,128)(2,1)} fusion(bf16[768,768]{1,0:T(8,128)(2,1)} %all-gather.5.cloned.1.call-done, f32[512,768]{1,0:T(8,128)S(1)} %get-tuple-element.253, f32[768]{0:T(1024)S(1)} %copy-done.15, f32[512]{0:T(512)S(1)} %add_rsqrt_fusion, f32[512]{0:T(512)S(1)} %broadcast_multiply_fusion), kind=kOutput, calls=%fused_computation.72 | convolution fusion | flops 606339072 | bytes 3546112 | tf_op jit(solution)/shard_map/dot_general | solution.py:142
  102.8 1.4 copy.1419
  104.2 1.6 copy.1422
  105.9 1.7 fusion.77
  107.5 2.4 fusion.82
  117.5 2.4 fusion.79
  127.7 3.0 %fusion.81 = (bf16[1,128,1,64]{3,2,1,0:T(2,128)(2,1)S(1)}, bf16[1,128,1,64]{3,2,1,0:T(2,128)(2,1)S(1)}, bf16[1,128,1,64]{3,2,1,0:T(2,128)(2,1)S(1)}, bf16[1,128,...) fusion(bf16[12,128,4,64]{3,2,1,0:T(4,128)(2,1)} %bitcast.349), kind=kLoop, calls=%fused_computation.224 | loop fusion | bytes 393216 | tf_op jit(solution)/shard_map/slice | solution.py:99
  132.1 1.5 copy.1512
  133.6 1.5 copy.1513
  148.3 3.4 %collective-permute-start.2 = (bf16[2,12,128,64]{2,3,1,0:T(8,128)(2,1)S(1)}, bf16[2,12,128,64]{2,3,1,0:T(8,128)(2,1)S(1)}, u32[]{:S(2)}, u32[]{:S(2)}) collective-permute-start(bf16[2,12,128,64]{2,3,1,0:T(8,128)(2,1)S(1)} %pad_maximum_fusion.2), channel_id=1, source_target_pairs={{0,1},{1,0},{2,3},{3,2},{4,5},{5,4},{6,7},{7,6},{8,9},{9,8},{10,11... | collective-permute-start | bytes 1179656 | tf_op jit(solution)/shard_map/ppermute | solution.py:37
  152.3 9.9 %collective-permute-done.2 = bf16[2,12,128,64]{2,3,1,0:T(8,128)(2,1)S(1)} collective-permute-done((bf16[2,12,128,64]{2,3,1,0:T(8,128)(2,1)S(1)}, bf16[2,12,128,64]{2,3,1,0:T(8,128)(2,1)S(1)}, u32[]{:S(2)}, u32[]{:S(2)}) %collective-permute-start.2) | collective-permute-done | bytes 393248 | tf_op jit(solution)/shard_map/ppermute | solution.py:37
  163.4 4.9 %collective-permute-start.3 = (bf16[2,12,256,64]{2,3,1,0:T(8,128)(2,1)}, bf16[2,12,256,64]{2,3,1,0:T(8,128)(2,1)}, u32[]{:S(2)}, u32[]{:S(2)}) collective-permute-start(bf16[2,12,256,64]{2,3,1,0:T(8,128)(2,1)} %maximum_select_fusion.1), channel_id=1, source_target_pairs={{0,2},{2,0},{1,3},{3,1},{4,6},{6,4},{5,7},{7,5},{8,10},{10,8},{9,1... | collective-permute-start | bytes 2359304 | tf_op jit(solution)/shard_map/ppermute | solution.py:37
  168.4 13.2 %while.10 = (s32[]{:T(128)}, f32[3,4,512]{2,1,0:T(4,128)S(1)}, f32[3,4,512]{2,1,0:T(4,128)S(1)}, f32[3,4,512,64]{2,3,1,0:T(8,128)}, pred[3,4,512]{2,1,0:T(4,128)...) while((s32[]{:T(128)}, f32[3,4,512]{2,1,0:T(4,128)S(1)}, ...), condition=%wide.region_5.6_spmd, body=%wide.region_2.5_spmd.sunk | while | flops 276965376 | bytes 14004325 | solution.py:88
  168.5 1.5 select_reduce_fusion.2
  170.0 1.9 fusion.105
  172.9 1.5 select_reduce_fusion.2
  174.4 1.9 fusion.105
  177.2 1.5 select_reduce_fusion.2
  178.8 1.9 fusion.105
  182.9 2.1 copy.1481
  185.0 27.4 %collective-permute-done.3 = bf16[2,12,256,64]{2,3,1,0:T(8,128)(2,1)} collective-permute-done((bf16[2,12,256,64]{2,3,1,0:T(8,128)(2,1)}, bf16[2,12,256,64]{2,3,1,0:T(8,128)(2,1)}, u32[]{:S(2)}, u32[]{:S(2)}) %collective-permute-start.3) | collective-permute-done | bytes 786464 | tf_op jit(solution)/shard_map/ppermute | solution.py:37
  212.3 2.6 maximum_select_fusion
  216.2 11.3 %while.11 = (s32[]{:T(128)}, f32[3,4,128]{2,1,0:T(4,128)S(1)}, f32[3,4,128]{2,1,0:T(4,128)S(1)}, f32[3,4,128,64]{2,3,1,0:T(8,128)}, pred[3,4,512]{2,1,0:T(4,128)...) while((s32[]{:T(128)}, f32[3,4,128]{2,1,0:T(4,128)S(1)}, ...), condition=%wide.region_9.10_spmd, body=%wide.region_6.9_spmd.sunk | while | flops 68717056 | bytes 3899493 | solution.py:88
  216.2 1.4 fusion.108
  217.6 2.0 fusion.111
  220.0 1.4 fusion.108
  221.4 2.0 fusion.111
  223.7 1.4 fusion.108
  225.1 2.0 fusion.111
  230.6 9.3 %fusion.74 = (bf16[1,12,512,64]{3,0,1,2:T(2,128)(2,1)}, bf16[1,12,512,64]{3,0,1,2:T(2,128)(2,1)}) fusion(bf16[2,12,512,64]{3,0,1,2:T(2,128)(2,1)} %all-gather.9.cloned.1.call-done), kind=kLoop, calls=%fused_computation.217 | loop fusion | bytes 3145728 | tf_op jit(solution)/shard_map/slice | solution.py:204
  239.9 7.9 %copy.1535 = bf16[1,12,512,64]{2,3,1,0:T(8,128)(2,1)} copy(bf16[1,12,512,64]{3,0,1,2:T(2,128)(2,1)} %get-tuple-element.267) | data formatting | bytes 1572864
  247.8 7.9 %copy.1536 = bf16[1,12,512,64]{2,3,1,0:T(8,128)(2,1)} copy(bf16[1,12,512,64]{3,0,1,2:T(2,128)(2,1)} %get-tuple-element.266) | data formatting | bytes 1572864
  255.7 1.4 fusion.84
  258.8 1.6 broadcast_in_dim.237
  261.3 1.5 fusion.58
  263.6 8.3 %fusion.52 = bf16[12,512,64]{2,1,0:T(8,128)(2,1)} fusion(f32[12,512,64]{2,1,0:T(8,128)S(1)} %bitcast.338, f32[3,4,512,64]{3,2,1,0:T(8,128)S(1)} %copy.1481, f32[12,512]{1,0:T(8,128)S(1)} %get-tuple-element.248, f32[12,16,64]{2,1,0:T(8,128)S(1)} %fusion.58, f32[12,512]{1,0:T(8,128)S(1)} %get-tuple-element.251, f32[12,512]{1,0:T(8,128)S(1)} %get-tuple-element.249, ...), kind=kLoop, calls=%fused_computation.63 | loop fusion | flops 4325376 | bytes 4116992 | tf_op jit(solution)/shard_map/convert_element_type | solution.py:221
  272.0 1.7 copy.1485
  273.7 3.0 %fusion.57 = bf16[1,512,768]{2,1,0:T(8,128)(2,1)} fusion(bf16[512,768]{0,1:T(8,128)(2,1)S(1)} %bitcast.359, bf16[768,768]{1,0:T(8,128)(2,1)} %all-gather.11.cloned.1.call-done), kind=kOutput, calls=%fused_computation.76 | convolution fusion | flops 604372992 | bytes 2752512 | tf_op jit(solution)/shard_map/dot_general | solution.py:223
  (225 shorter events, 53.4 us)
Async XLA Ops:
  6.5 9.0 %copy-start.9 = (f32[5,768]{1,0:T(8,128)S(1)}, f32[5,768]{1,0:T(8,128)}, u32[]{:S(2)}) copy-start(f32[5,768]{1,0:T(8,128)} %param.13) | copy-start | bytes 46084
  6.5 51.2 %all-gather.7.cloned.1.call-start = ((), (), s32[]{:S(2)}) async-start(), calls=%async_computation.1 | async-start | bytes 2506752 | tf_op jit(solution)/shard_map/all_gather | solution.py:139
  7.3 92.6 %all-gather.5.cloned.1.call-start = ((), (), s32[]{:S(2)}) async-start(), calls=%async_computation | async-start | bytes 1253376 | tf_op jit(solution)/shard_map/all_gather | solution.py:138
  8.0 7.5 %copy-start.12 = (pred[512]{0:T(512)(128)(4,1)}, pred[512]{0:T(512)(128)(4,1)S(1)}, u32[]{:S(2)}) copy-start(pred[512]{0:T(512)(128)(4,1)S(1)} %add_compare_fusion.2) | copy-start | bytes 1540
  9.3 6.3 %collective-permute-start = (bf16[6,768]{1,0:T(8,128)(2,1)S(1)}, bf16[6,768]{1,0:T(8,128)(2,1)S(1)}, u32[]{:S(2)}, u32[]{:S(2)}) collective-permute-start(bf16[6,768]{1,0:T(8,128)(2,1)S(1)} %get-tuple-element.344), channel_id=1, source_target_pairs={{0,1},{1,2},{2,3},{3,4},{4,5},{5,6},{6,7},{7,8},{8,9},{9,10},{10,1... | collective-permute-start | bytes 27656 | tf_op jit(solution)/shard_map/ppermute | solution.py:21
  14.1 5.1 %collective-permute-start.1 = (bf16[6,768]{1,0:T(8,128)(2,1)S(1)}, bf16[6,768]{1,0:T(8,128)(2,1)S(1)}, u32[]{:S(2)}, u32[]{:S(2)}) collective-permute-start(bf16[6,768]{1,0:T(8,128)(2,1)S(1)} %get-tuple-element.345), channel_id=1, source_target_pairs={{1,0},{2,1},{3,2},{4,3},{5,4},{6,5},{7,6},{8,7},{9,8},{10,9},{11,1... | collective-permute-start | bytes 27656 | tf_op jit(solution)/shard_map/ppermute | solution.py:23
  15.4 215.2 %all-gather.9.cloned.1.call-start = ((), (), s32[]{:S(2)}) async-start(), calls=%async_computation.2 | async-start | bytes 3244032 | tf_op jit(solution)/shard_map/all_gather | solution.py:197
  19.2 38.6 %copy-start.15 = (f32[768]{0:T(1024)S(1)}, f32[768]{0:T(1024)}, u32[]{:S(2)}) copy-start(f32[768]{0:T(1024)} %param.14) | copy-start | bytes 9220
  69.9 203.8 %all-gather.11.cloned.1.call-start = ((), (), s32[]{:S(2)}) async-start(), calls=%async_computation.3 | async-start | bytes 1253376 | tf_op jit(solution)/shard_map/all_gather | solution.py:225
  117.4 2.5 copy-start.4
  135.9 16.4 %copy-start.3 = (bf16[1,128,1,64]{1,3,2,0:T(8,128)(2,1)S(1)}, bf16[1,128,1,64]{1,3,2,0:T(8,128)(2,1)}, u32[]{:S(2)}) copy-start(bf16[1,128,1,64]{1,3,2,0:T(8,128)(2,1)} %copy.1434) | copy-start | bytes 49156
  136.6 15.1 %copy-start.6 = (bf16[1,16,1,64]{3,2,1,0:T(2,128)(2,1)S(1)}, bf16[1,16,1,64]{3,2,1,0:T(2,128)(2,1)}, u32[]{:S(2)}) copy-start(bf16[1,16,1,64]{3,2,1,0:T(2,128)(2,1)} %get-tuple-element.292) | copy-start | bytes 6148
  137.3 31.1 %copy-start.13 = (pred[512]{0:T(512)(128)(4,1)S(1)}, pred[512]{0:T(512)(128)(4,1)}, u32[]{:S(2)}) copy-start(pred[512]{0:T(512)(128)(4,1)} %copy-done.12) | copy-start | bytes 1540
  137.3 31.1 %copy-start.7 = (f32[3,4,512]{2,1,0:T(4,128)S(1)}, f32[3,4,512]{2,1,0:T(4,128)}, u32[]{:S(2)}) copy-start(f32[3,4,512]{2,1,0:T(4,128)} %custom-call.6) | copy-start | bytes 73732
  137.3 31.1 %copy-start.8 = (f32[3,4,512]{2,1,0:T(4,128)S(1)}, f32[3,4,512]{2,1,0:T(4,128)}, u32[]{:S(2)}) copy-start(f32[3,4,512]{2,1,0:T(4,128)} %custom-call.7) | copy-start | bytes 73732
  148.3 13.9 %collective-permute-start.2 = (bf16[2,12,128,64]{2,3,1,0:T(8,128)(2,1)S(1)}, bf16[2,12,128,64]{2,3,1,0:T(8,128)(2,1)S(1)}, u32[]{:S(2)}, u32[]{:S(2)}) collective-permute-start(bf16[2,12,128,64]{2,3,1,0:T(8,128)(2,1)S(1)} %pad_maximum_fusion.2), channel_id=1, source_target_pairs={{0,1},{1,0},{2,3},{3,2},{4,5},{5,4},{6,7},{7,6},{8,9},{9,8},{10,11... | collective-permute-start | bytes 1179656 | tf_op jit(solution)/shard_map/ppermute | solution.py:37
  163.4 48.9 %collective-permute-start.3 = (bf16[2,12,256,64]{2,3,1,0:T(8,128)(2,1)}, bf16[2,12,256,64]{2,3,1,0:T(8,128)(2,1)}, u32[]{:S(2)}, u32[]{:S(2)}) collective-permute-start(bf16[2,12,256,64]{2,3,1,0:T(8,128)(2,1)} %maximum_select_fusion.1), channel_id=1, source_target_pairs={{0,2},{2,0},{1,3},{3,1},{4,6},{6,4},{5,7},{7,5},{8,10},{10,8},{9,1... | collective-permute-start | bytes 2359304 | tf_op jit(solution)/shard_map/ppermute | solution.py:37
  214.9 1.3 copy-start.10
  214.9 1.3 copy-start.11
  247.8 7.9 %copy-start.5 = (pred[12,512]{1,0:T(8,128)(4,1)S(1)}, pred[12,512]{1,0:T(8,128)(4,1)}, u32[]{:S(2)}) copy-start(pred[12,512]{1,0:T(8,128)(4,1)} %add_compare_fusion) | copy-start | bytes 18436
  260.4 2.5 copy-start
  262.9 0.8 copy-start.1
  262.9 0.8 copy-start.2
  262.9 0.7 copy-start.14
Sparse Core Ops, SparseCore 0:
  9.5 48.2 all-gather.6
  59.9 39.9 all-gather.4
  103.0 101.3 all-gather.8
  206.4 41.1 all-gather.10
where the time goes:
time: 286 us; the launch traced here: 283 us
  waiting for transfers between devices  107 us (37%)
  local copies, waits for them, and re-layouts  92.1 us (32%)
  matrix products  32.4 us (11%)
  other arithmetic  22.6 us (8%)
  between operations  14.6 us (5%)
  starting transfers between devices  14.5 us (5%)
    unnamed x112, local copies, waits for them, and re-layouts  38.8 us
    ppermute x2, waiting for transfers between devices, partner_2(): return lax.ppermute(block, axis, route)  37.3 us
    all_gather x1, waiting for transfers between devices, on_device(): lax.all_gather(w_keyvalue, 'batch', axis=0, tiled=True)  37.1 us
    all_gather x1, waiting for transfers between devices, on_device(): lax.all_gather(w_query, 'batch', axis=0, tiled=True)  27.5 us
    slice x30, local copies, waits for them, and re-layouts, pick_rows(): grouped[head, :, head % rate, :]  21 us
    dot_general x7, matrix products, update(): jnp.einsum('hcp,hpu->hcu', exponent.astype(jnp.bfloat16), value_block, pr...  13.2 us
    dot_general x7, matrix products, update(): jnp.einsum('ftl,fhl->fth', query_segment_block, key_segment_block, prefer...  10.1 us
    slice x1, local copies, waits for them, and re-layouts, on_device(): piece_rows[1]  9.28 us
  transfers between devices with their start and end apart: 8, of which 5 were waited for; matrix products, arithmetic and copies ran while one was open for 51% of the time, Pallas kernels for 0%

commit v1 on v0

--- a/solution.py
+++ b/solution.py
@@ -8,6 +8,22 @@
 GROUP = 4
 CONV_TAP_COUNT = 5
 CONV_DILATION = 3
+
+
+def collect(x, axis, dim):
+    ways, here, step = (lax.axis_size(axis), lax.axis_index(axis), x.shape[dim])
+    shape = [n * ways if d == dim else n for d, n in enumerate(x.shape)]
+    full = lax.dynamic_update_slice_in_dim(jnp.zeros(shape, x.dtype), x, here * step, axis=dim)
+    going_up = going_down = x
+    for far in range(1, ways // 2 + 1):
+        going_up = lax.ppermute(going_up, axis, [(d, (d + 1) % ways) for d in range(ways)])
+        full = lax.dynamic_update_slice_in_dim(full, going_up, (here - far) % ways * step, axis=dim)
+        if 2 * far < ways:
+            going_down = lax.ppermute(going_down, axis, [(d, (d - 1) % ways) for d in range(ways)])
+            full = lax.dynamic_update_slice_in_dim(
+                full, going_down, (here + far) % ways * step, axis=dim
+            )
+    return full
 
 
 def with_halo(cells, sides, width):
@@ -135,7 +151,7 @@
     variance = jnp.mean(centered * centered, axis=-1, keepdims=True)
     normed = (centered * lax.rsqrt(variance + 1e-05) * norm_gain).astype(jnp.bfloat16)
     piece_rows = (
-        lax.all_gather(w_query, "batch", axis=0, tiled=True),
+        collect(w_query, "batch", 0),
         lax.all_gather(w_keyvalue, "batch", axis=0, tiled=True),
     )
     columns = normed

time: 286 us -> 276 us (0.965)
  waiting for transfers between devices: 107 us -> 73.7 us
  starting transfers between devices: 14.5 us -> 37.5 us
    all_gather x1 -> x0, waiting for transfers between devices: 27.5 us -> none  [on_device(): lax.all_gather(w_query, 'batch', axis=0, tiled=True)]
    ppermute x0 -> x15, starting transfers between devices: none -> 23.8 us  [the longest x7 16.7 us: collect(): lax.ppermute(going_down, axis, [(d, (d - 1) % ways) for d in range(ways)])]
    ppermute x2, waiting for transfers between devices: 37.3 us -> 22.2 us  [partner_2(): return lax.ppermute(block, axis, route)]
    ppermute x0 -> x15, waiting for transfers between devices: none -> 9.92 us  [the longest x8 9.45 us: collect(): lax.ppermute(going_up, axis, [(d, (d + 1) % ways) for d in range(ways)])]
    unnamed x112 -> x114, local copies, waits for them, and re-layouts: 38.8 us -> 38.8 us
  transfers between devices with their start and end apart: 8 -> 22, of which waited for: 5 -> 14; matrix products, arithmetic and copies ran while one was open for 51% -> 48% of each run, Pallas kernels for 0% -> 0%
where the time goes in v1:
time: 276 us; the launch traced here: 273 us
  local copies, waits for them, and re-layouts  92.7 us (34%)
  waiting for transfers between devices  73.7 us (27%)
  starting transfers between devices  37.5 us (14%)
  matrix products  31.1 us (11%)
  other arithmetic  22.4 us (8%)
  between operations  15.1 us (5%)
    unnamed x114, local copies, waits for them, and re-layouts  38.8 us
    all_gather x1, waiting for transfers between devices, on_device(): lax.all_gather(w_keyvalue, 'batch', axis=0, tiled=True)  37.1 us
    ppermute x2, waiting for transfers between devices, partner_2(): return lax.ppermute(block, axis, route)  22.2 us
    slice x30, local copies, waits for them, and re-layouts, pick_rows(): grouped[head, :, head % rate, :]  21.2 us
    ppermute x7, starting transfers between devices, collect(): lax.ppermute(going_down, axis, [(d, (d - 1) % ways) for d in range(ways)])  16.7 us
    dot_general x7, matrix products, update(): jnp.einsum('hcp,hpu->hcu', exponent.astype(jnp.bfloat16), value_block, pr...  13.2 us
    dot_general x7, matrix products, update(): jnp.einsum('ftl,fhl->fth', query_segment_block, key_segment_block, prefer...  10.1 us
    ppermute x8, waiting for transfers between devices, collect(): lax.ppermute(going_up, axis, [(d, (d + 1) % ways) for d in range(ways)])  9.45 us
  transfers between devices with their start and end apart: 22, of which 14 were waited for; matrix products, arithmetic and copies ran while one was open for 48% of the time, Pallas kernels for 0%

profile of v1, /device:TPU:1, one launch (start us, length us, event | category | flops | bytes accessed | tf_op | source)
XLA Modules:
  0.0 272.6 jit_solution(17923962602906898053)
XLA Ops:
  9.3 4.8 %collective-permute-start = (bf16[6,768]{1,0:T(8,128)(2,1)S(1)}, bf16[6,768]{1,0:T(8,128)(2,1)S(1)}, u32[]{:S(2)}, u32[]{:S(2)}) collective-permute-start(bf16[6,768]{1,0:T(8,128)(2,1)S(1)} %get-tuple-element.344), channel_id=1, source_target_pairs={{0,1},{1,2},{2,3},{3,4},{4,5},{5,6},{6,7},{7,8},{8,9},{9,10},{10,1... | collective-permute-start | bytes 27656 | tf_op jit(solution)/shard_map/ppermute | solution.py:37
  15.5 3.7 %collective-permute-done.1 = bf16[6,768]{1,0:T(8,128)(2,1)S(1)} collective-permute-done((bf16[6,768]{1,0:T(8,128)(2,1)S(1)}, bf16[6,768]{1,0:T(8,128)(2,1)S(1)}, u32[]{:S(2)}, u32[]{:S(2)}) %collective-permute-start.1) | collective-permute-done | bytes 9248 | tf_op jit(solution)/shard_map/ppermute | solution.py:39
  20.7 37.1 %all-gather.4.cloned.1.call-done = bf16[768,1536]{1,0:T(8,128)(2,1)} async-done(((bf16[48,1536]{1,0:T(8,128)(2,1)}), bf16[768,1536]{1,0:T(8,128)(2,1)}) %all-gather.4.cloned.1.call-update) | async-done | bytes 2359312 | tf_op jit(solution)/shard_map/all_gather | solution.py:155
  57.8 3.1 %convolution_convert_fusion = bf16[512,1536]{1,0:T(8,128)(2,1)S(1)} fusion(bf16[768,1536]{1,0:T(8,128)(2,1)} %all-gather.4.cloned.1.call-done, f32[512,768]{1,0:T(8,128)S(1)} %get-tuple-element.253, f32[768]{0:T(1024)S(1)} %copy-done.16, f32[512]{0:T(512)S(1)} %add_rsqrt_fusion, f32[512]{0:T(512)S(1)} %broadcast_multiply_fusion), kind=kOutput, calls=%fused_computation.64 | convolution fusion | flops 1210318848 | bytes 5512192 | tf_op jit(solution)/shard_map/dot_general | solution.py:159
  62.2 1.5 copy.1435
  66.2 1.6 copy.1448
  73.5 1.8 collective-permute-start.4
  76.6 2.4 collective-permute-start.6
  79.0 1.5 collective-permute-start.7
  81.3 1.5 collective-permute-start.8
  82.8 2.7 %collective-permute-start.9 = (bf16[48,768]{1,0:T(8,128)(2,1)S(1)}, bf16[48,768]{1,0:T(8,128)(2,1)S(1)}, u32[]{:S(2)}, u32[]{:S(2)}) collective-permute-start(bf16[48,768]{1,0:T(8,128)(2,1)S(1)} %collective-permute-done.7), channel_id=1, source_target_pairs={{0,480},{32,0},{64,32},{96,64},{128,96},{160,128},{192,160},{224,1... | collective-permute-start | bytes 221192 | tf_op jit(solution)/shard_map/ppermute | solution.py:22
  86.6 3.9 %collective-permute-start.11 = (bf16[48,768]{1,0:T(8,128)(2,1)S(1)}, bf16[48,768]{1,0:T(8,128)(2,1)S(1)}, u32[]{:S(2)}, u32[]{:S(2)}) collective-permute-start(bf16[48,768]{1,0:T(8,128)(2,1)S(1)} %collective-permute-done.9), channel_id=1, source_target_pairs={{0,480},{32,0},{64,32},{96,64},{128,96},{160,128},{192,160},{224,1... | collective-permute-start | bytes 221192 | tf_op jit(solution)/shard_map/ppermute | solution.py:22
  91.4 4.1 %collective-permute-start.13 = (bf16[48,768]{1,0:T(8,128)(2,1)S(1)}, bf16[48,768]{1,0:T(8,128)(2,1)S(1)}, u32[]{:S(2)}, u32[]{:S(2)}) collective-permute-start(bf16[48,768]{1,0:T(8,128)(2,1)S(1)} %collective-permute-done.11), channel_id=1, source_target_pairs={{0,480},{32,0},{64,32},{96,64},{128,96},{160,128},{192,160},{224,1... | collective-permute-start | bytes 221192 | tf_op jit(solution)/shard_map/ppermute | solution.py:22
  96.4 4.1 %collective-permute-start.15 = (bf16[48,768]{1,0:T(8,128)(2,1)S(1)}, bf16[48,768]{1,0:T(8,128)(2,1)S(1)}, u32[]{:S(2)}, u32[]{:S(2)}) collective-permute-start(bf16[48,768]{1,0:T(8,128)(2,1)S(1)} %collective-permute-done.13), channel_id=1, source_target_pairs={{0,480},{32,0},{64,32},{96,64},{128,96},{160,128},{192,160},{224,1... | collective-permute-start | bytes 221192 | tf_op jit(solution)/shard_map/ppermute | solution.py:22
  101.4 4.8 %collective-permute-done.16 = bf16[48,768]{1,0:T(8,128)(2,1)S(1)} collective-permute-done((bf16[48,768]{1,0:T(8,128)(2,1)S(1)}, bf16[48,768]{1,0:T(8,128)(2,1)S(1)}, u32[]{:S(2)}, u32[]{:S(2)}) %collective-permute-start.16) | collective-permute-done | bytes 73760 | tf_op jit(solution)/shard_map/ppermute | solution.py:19
  106.2 1.7 multiply_convert_fusion
  109.4 1.6 copy.1422
  111.0 1.7 fusion.77
  112.7 2.4 fusion.82
  122.7 2.6 fusion.79
  133.0 3.0 %fusion.81 = (bf16[1,128,1,64]{3,2,1,0:T(2,128)(2,1)S(1)}, bf16[1,128,1,64]{3,2,1,0:T(2,128)(2,1)S(1)}, bf16[1,128,1,64]{3,2,1,0:T(2,128)(2,1)S(1)}, bf16[1,128,...) fusion(bf16[12,128,4,64]{3,2,1,0:T(4,128)(2,1)} %bitcast.349), kind=kLoop, calls=%fused_computation.240 | loop fusion | bytes 393216 | tf_op jit(solution)/shard_map/slice | solution.py:115
  137.5 1.5 copy.1512
  139.0 1.5 copy.1513
  153.7 3.3 %collective-permute-start.17 = (bf16[2,12,128,64]{2,3,1,0:T(8,128)(2,1)S(1)}, bf16[2,12,128,64]{2,3,1,0:T(8,128)(2,1)S(1)}, u32[]{:S(2)}, u32[]{:S(2)}) collective-permute-start(bf16[2,12,128,64]{2,3,1,0:T(8,128)(2,1)S(1)} %pad_maximum_fusion.2), channel_id=1, source_target_pairs={{0,1},{1,0},{2,3},{3,2},{4,5},{5,4},{6,7},{7,6},{8,9},{9,8},{10,11... | collective-permute-start | bytes 1179656 | tf_op jit(solution)/shard_map/ppermute | solution.py:53
  157.6 4.8 %collective-permute-done.17 = bf16[2,12,128,64]{2,3,1,0:T(8,128)(2,1)S(1)} collective-permute-done((bf16[2,12,128,64]{2,3,1,0:T(8,128)(2,1)S(1)}, bf16[2,12,128,64]{2,3,1,0:T(8,128)(2,1)S(1)}, u32[]{:S(2)}, u32[]{:S(2)}) %collective-permute-start.17) | collective-permute-done | bytes 393248 | tf_op jit(solution)/shard_map/ppermute | solution.py:53
  163.6 4.2 %collective-permute-start.18 = (bf16[2,12,256,64]{2,3,1,0:T(8,128)(2,1)}, bf16[2,12,256,64]{2,3,1,0:T(8,128)(2,1)}, u32[]{:S(2)}, u32[]{:S(2)}) collective-permute-start(bf16[2,12,256,64]{2,3,1,0:T(8,128)(2,1)} %maximum_select_fusion.1), channel_id=1, source_target_pairs={{0,2},{2,0},{1,3},{3,1},{4,6},{6,4},{5,7},{7,5},{8,10},{10,8},{9,1... | collective-permute-start | bytes 2359304 | tf_op jit(solution)/shard_map/ppermute | solution.py:53
  167.8 13.2 %while.10 = (s32[]{:T(128)}, f32[3,4,512]{2,1,0:T(4,128)S(1)}, f32[3,4,512]{2,1,0:T(4,128)S(1)}, f32[3,4,512,64]{2,3,1,0:T(8,128)}, pred[3,4,512]{2,1,0:T(4,128)...) while((s32[]{:T(128)}, f32[3,4,512]{2,1,0:T(4,128)S(1)}, ...), condition=%wide.region_5.6_spmd, body=%wide.region_2.5_spmd.sunk | while | flops 276965376 | bytes 14004325 | solution.py:104
  167.9 1.5 select_reduce_fusion.2
  169.4 1.9 fusion.105
  172.3 1.5 select_reduce_fusion.2
  173.8 1.9 fusion.105
  176.7 1.5 select_reduce_fusion.2
  178.2 1.9 fusion.105
  182.3 2.1 copy.1481
  184.5 17.5 %collective-permute-done.18 = bf16[2,12,256,64]{2,3,1,0:T(8,128)(2,1)} collective-permute-done((bf16[2,12,256,64]{2,3,1,0:T(8,128)(2,1)}, bf16[2,12,256,64]{2,3,1,0:T(8,128)(2,1)}, u32[]{:S(2)}, u32[]{:S(2)}) %collective-permute-start.18) | collective-permute-done | bytes 786464 | tf_op jit(solution)/shard_map/ppermute | solution.py:53
  201.9 2.4 maximum_select_fusion
  205.6 11.3 %while.11 = (s32[]{:T(128)}, f32[3,4,128]{2,1,0:T(4,128)S(1)}, f32[3,4,128]{2,1,0:T(4,128)S(1)}, f32[3,4,128,64]{2,3,1,0:T(8,128)}, pred[3,4,512]{2,1,0:T(4,128)...) while((s32[]{:T(128)}, f32[3,4,128]{2,1,0:T(4,128)S(1)}, ...), condition=%wide.region_9.10_spmd, body=%wide.region_6.9_spmd.sunk | while | flops 68717056 | bytes 3899493 | solution.py:104
  207.0 2.0 fusion.111
  210.8 2.0 fusion.111
  214.6 2.0 fusion.111
  220.0 9.4 %fusion.74 = (bf16[1,12,512,64]{3,0,1,2:T(2,128)(2,1)}, bf16[1,12,512,64]{3,0,1,2:T(2,128)(2,1)}) fusion(bf16[2,12,512,64]{3,0,1,2:T(2,128)(2,1)} %all-gather.6.cloned.1.call-done), kind=kLoop, calls=%fused_computation.233 | loop fusion | bytes 3145728 | tf_op jit(solution)/shard_map/slice | solution.py:220
  229.4 7.9 %copy.1535 = bf16[1,12,512,64]{2,3,1,0:T(8,128)(2,1)} copy(bf16[1,12,512,64]{3,0,1,2:T(2,128)(2,1)} %get-tuple-element.267) | data formatting | bytes 1572864
  237.3 7.9 %copy.1536 = bf16[1,12,512,64]{2,3,1,0:T(8,128)(2,1)} copy(bf16[1,12,512,64]{3,0,1,2:T(2,128)(2,1)} %get-tuple-element.266) | data formatting | bytes 1572864
  248.3 1.6 broadcast_in_dim.241
  250.8 1.5 fusion.58
  253.1 8.3 %fusion.52 = bf16[12,512,64]{2,1,0:T(8,128)(2,1)} fusion(f32[12,512,64]{2,1,0:T(8,128)S(1)} %bitcast.338, f32[3,4,512,64]{3,2,1,0:T(8,128)S(1)} %copy.1481, f32[12,512]{1,0:T(8,128)S(1)} %get-tuple-element.248, f32[12,16,64]{2,1,0:T(8,128)S(1)} %fusion.58, f32[12,512]{1,0:T(8,128)S(1)} %get-tuple-element.251, f32[12,512]{1,0:T(8,128)S(1)} %get-tuple-element.249, ...), kind=kLoop, calls=%fused_computation.63 | loop fusion | flops 4325376 | bytes 4116992 | tf_op jit(solution)/shard_map/convert_element_type | solution.py:237
  261.4 1.7 copy.1485
  263.2 3.0 %fusion.57 = bf16[1,512,768]{2,1,0:T(8,128)(2,1)} fusion(bf16[512,768]{0,1:T(8,128)(2,1)S(1)} %bitcast.359, bf16[768,768]{1,0:T(8,128)(2,1)} %all-gather.8.cloned.1.call-done), kind=kOutput, calls=%fused_computation.76 | convolution fusion | flops 604372992 | bytes 2752512 | tf_op jit(solution)/shard_map/dot_general | solution.py:239
  (271 shorter events, 71.0 us)
Async XLA Ops:
  6.5 8.9 %copy-start.10 = (f32[5,768]{1,0:T(8,128)S(1)}, f32[5,768]{1,0:T(8,128)}, u32[]{:S(2)}) copy-start(f32[5,768]{1,0:T(8,128)} %param.13) | copy-start | bytes 46084
  6.5 51.2 %all-gather.4.cloned.1.call-start = ((), (), s32[]{:S(2)}) async-start(), calls=%async_computation | async-start | bytes 2506752 | tf_op jit(solution)/shard_map/all_gather | solution.py:155
  7.3 212.8 %all-gather.6.cloned.1.call-start = ((), (), s32[]{:S(2)}) async-start(), calls=%async_computation.1 | async-start | bytes 3244032 | tf_op jit(solution)/shard_map/all_gather | solution.py:213
  8.0 11.2 %copy-start.13 = (pred[512]{0:T(512)(128)(4,1)}, pred[512]{0:T(512)(128)(4,1)S(1)}, u32[]{:S(2)}) copy-start(pred[512]{0:T(512)(128)(4,1)S(1)} %add_compare_fusion.2) | copy-start | bytes 1540
  9.3 6.2 %collective-permute-start = (bf16[6,768]{1,0:T(8,128)(2,1)S(1)}, bf16[6,768]{1,0:T(8,128)(2,1)S(1)}, u32[]{:S(2)}, u32[]{:S(2)}) collective-permute-start(bf16[6,768]{1,0:T(8,128)(2,1)S(1)} %get-tuple-element.344), channel_id=1, source_target_pairs={{0,1},{1,2},{2,3},{3,4},{4,5},{5,6},{6,7},{7,8},{8,9},{9,10},{10,1... | collective-permute-start | bytes 27656 | tf_op jit(solution)/shard_map/ppermute | solution.py:37
  14.1 5.1 %collective-permute-start.1 = (bf16[6,768]{1,0:T(8,128)(2,1)S(1)}, bf16[6,768]{1,0:T(8,128)(2,1)S(1)}, u32[]{:S(2)}, u32[]{:S(2)}) collective-permute-start(bf16[6,768]{1,0:T(8,128)(2,1)S(1)} %get-tuple-element.345), channel_id=1, source_target_pairs={{1,0},{2,1},{3,2},{4,3},{5,4},{6,5},{7,6},{8,7},{9,8},{10,9},{11,1... | collective-permute-start | bytes 27656 | tf_op jit(solution)/shard_map/ppermute | solution.py:39
  19.2 38.6 %copy-start.16 = (f32[768]{0:T(1024)S(1)}, f32[768]{0:T(1024)}, u32[]{:S(2)}) copy-start(f32[768]{0:T(1024)} %param.14) | copy-start | bytes 9220
  66.2 3.7 %copy-start.2 = (bf16[48,768]{1,0:T(8,128)(2,1)S(1)}, bf16[48,768]{1,0:T(8,128)(2,1)}, u32[]{:S(2)}) copy-start(bf16[48,768]{1,0:T(8,128)(2,1)} %param.15) | copy-start | bytes 221188
  69.9 193.3 %all-gather.8.cloned.1.call-start = ((), (), s32[]{:S(2)}) async-start(), calls=%async_computation.2 | async-start | bytes 1253376 | tf_op jit(solution)/shard_map/all_gather | solution.py:241
  69.9 3.5 %collective-permute-start.2 = (bf16[48,768]{1,0:T(8,128)(2,1)S(1)}, bf16[48,768]{1,0:T(8,128)(2,1)S(1)}, u32[]{:S(2)}, u32[]{:S(2)}) collective-permute-start(bf16[48,768]{1,0:T(8,128)(2,1)S(1)} %copy-done.2), channel_id=1, source_target_pairs={{0,32},{32,64},{64,96},{96,128},{128,160},{160,192},{192,224},{224... | collective-permute-start | bytes 221192 | tf_op jit(solution)/shard_map/ppermute | solution.py:19
  71.1 4.1 %collective-permute-start.3 = (bf16[48,768]{1,0:T(8,128)(2,1)S(1)}, bf16[48,768]{1,0:T(8,128)(2,1)S(1)}, u32[]{:S(2)}, u32[]{:S(2)}) collective-permute-start(bf16[48,768]{1,0:T(8,128)(2,1)S(1)} %copy-done.2), channel_id=1, source_target_pairs={{0,480},{32,0},{64,32},{96,64},{128,96},{160,128},{192,160},{224,1... | collective-permute-start | bytes 221192 | tf_op jit(solution)/shard_map/ppermute | solution.py:22
  73.5 3.2 %collective-permute-start.4 = (bf16[48,768]{1,0:T(8,128)(2,1)S(1)}, bf16[48,768]{1,0:T(8,128)(2,1)S(1)}, u32[]{:S(2)}, u32[]{:S(2)}) collective-permute-start(bf16[48,768]{1,0:T(8,128)(2,1)S(1)} %collective-permute-done.2), channel_id=1, source_target_pairs={{0,32},{32,64},{64,96},{96,128},{128,160},{160,192},{192,224},{224... | collective-permute-start | bytes 221192 | tf_op jit(solution)/shard_map/ppermute | solution.py:19
  75.2 3.8 %collective-permute-start.5 = (bf16[48,768]{1,0:T(8,128)(2,1)S(1)}, bf16[48,768]{1,0:T(8,128)(2,1)S(1)}, u32[]{:S(2)}, u32[]{:S(2)}) collective-permute-start(bf16[48,768]{1,0:T(8,128)(2,1)S(1)} %collective-permute-done.3), channel_id=1, source_target_pairs={{0,480},{32,0},{64,32},{96,64},{128,96},{160,128},{192,160},{224,1... | collective-permute-start | bytes 221192 | tf_op jit(solution)/shard_map/ppermute | solution.py:22
  76.6 4.6 %collective-permute-start.6 = (bf16[48,768]{1,0:T(8,128)(2,1)S(1)}, bf16[48,768]{1,0:T(8,128)(2,1)S(1)}, u32[]{:S(2)}, u32[]{:S(2)}) collective-permute-start(bf16[48,768]{1,0:T(8,128)(2,1)S(1)} %collective-permute-done.4), channel_id=1, source_target_pairs={{0,32},{32,64},{64,96},{96,128},{128,160},{160,192},{192,224},{224... | collective-permute-start | bytes 221192 | tf_op jit(solution)/shard_map/ppermute | solution.py:19
  79.0 3.8 %collective-permute-start.7 = (bf16[48,768]{1,0:T(8,128)(2,1)S(1)}, bf16[48,768]{1,0:T(8,128)(2,1)S(1)}, u32[]{:S(2)}, u32[]{:S(2)}) collective-permute-start(bf16[48,768]{1,0:T(8,128)(2,1)S(1)} %collective-permute-done.5), channel_id=1, source_target_pairs={{0,480},{32,0},{64,32},{96,64},{128,96},{160,128},{192,160},{224,1... | collective-permute-start | bytes 221192 | tf_op jit(solution)/shard_map/ppermute | solution.py:22
  81.3 5.0 %collective-permute-start.8 = (bf16[48,768]{1,0:T(8,128)(2,1)S(1)}, bf16[48,768]{1,0:T(8,128)(2,1)S(1)}, u32[]{:S(2)}, u32[]{:S(2)}) collective-permute-start(bf16[48,768]{1,0:T(8,128)(2,1)S(1)} %collective-permute-done.6), channel_id=1, source_target_pairs={{0,32},{32,64},{64,96},{96,128},{128,160},{160,192},{192,224},{224... | collective-permute-start | bytes 221192 | tf_op jit(solution)/shard_map/ppermute | solution.py:19
  82.8 3.8 %collective-permute-start.9 = (bf16[48,768]{1,0:T(8,128)(2,1)S(1)}, bf16[48,768]{1,0:T(8,128)(2,1)S(1)}, u32[]{:S(2)}, u32[]{:S(2)}) collective-permute-start(bf16[48,768]{1,0:T(8,128)(2,1)S(1)} %collective-permute-done.7), channel_id=1, source_target_pairs={{0,480},{32,0},{64,32},{96,64},{128,96},{160,128},{192,160},{224,1... | collective-permute-start | bytes 221192 | tf_op jit(solution)/shard_map/ppermute | solution.py:22
  86.3 5.0 %collective-permute-start.10 = (bf16[48,768]{1,0:T(8,128)(2,1)S(1)}, bf16[48,768]{1,0:T(8,128)(2,1)S(1)}, u32[]{:S(2)}, u32[]{:S(2)}) collective-permute-start(bf16[48,768]{1,0:T(8,128)(2,1)S(1)} %collective-permute-done.8), channel_id=1, source_target_pairs={{0,32},{32,64},{64,96},{96,128},{128,160},{160,192},{192,224},{224... | collective-permute-start | bytes 221192 | tf_op jit(solution)/shard_map/ppermute | solution.py:19
  86.6 4.9 %collective-permute-start.11 = (bf16[48,768]{1,0:T(8,128)(2,1)S(1)}, bf16[48,768]{1,0:T(8,128)(2,1)S(1)}, u32[]{:S(2)}, u32[]{:S(2)}) collective-permute-start(bf16[48,768]{1,0:T(8,128)(2,1)S(1)} %collective-permute-done.9), channel_id=1, source_target_pairs={{0,480},{32,0},{64,32},{96,64},{128,96},{160,128},{192,160},{224,1... | collective-permute-start | bytes 221192 | tf_op jit(solution)/shard_map/ppermute | solution.py:22
  91.3 5.0 %collective-permute-start.12 = (bf16[48,768]{1,0:T(8,128)(2,1)S(1)}, bf16[48,768]{1,0:T(8,128)(2,1)S(1)}, u32[]{:S(2)}, u32[]{:S(2)}) collective-permute-start(bf16[48,768]{1,0:T(8,128)(2,1)S(1)} %collective-permute-done.10), channel_id=1, source_target_pairs={{0,32},{32,64},{64,96},{96,128},{128,160},{160,192},{192,224},{224... | collective-permute-start | bytes 221192 | tf_op jit(solution)/shard_map/ppermute | solution.py:19
  91.4 5.0 %collective-permute-start.13 = (bf16[48,768]{1,0:T(8,128)(2,1)S(1)}, bf16[48,768]{1,0:T(8,128)(2,1)S(1)}, u32[]{:S(2)}, u32[]{:S(2)}) collective-permute-start(bf16[48,768]{1,0:T(8,128)(2,1)S(1)} %collective-permute-done.11), channel_id=1, source_target_pairs={{0,480},{32,0},{64,32},{96,64},{128,96},{160,128},{192,160},{224,1... | collective-permute-start | bytes 221192 | tf_op jit(solution)/shard_map/ppermute | solution.py:22
  96.2 5.0 %collective-permute-start.14 = (bf16[48,768]{1,0:T(8,128)(2,1)S(1)}, bf16[48,768]{1,0:T(8,128)(2,1)S(1)}, u32[]{:S(2)}, u32[]{:S(2)}) collective-permute-start(bf16[48,768]{1,0:T(8,128)(2,1)S(1)} %collective-permute-done.12), channel_id=1, source_target_pairs={{0,32},{32,64},{64,96},{96,128},{128,160},{160,192},{192,224},{224... | collective-permute-start | bytes 221192 | tf_op jit(solution)/shard_map/ppermute | solution.py:19
  96.4 5.0 %collective-permute-start.15 = (bf16[48,768]{1,0:T(8,128)(2,1)S(1)}, bf16[48,768]{1,0:T(8,128)(2,1)S(1)}, u32[]{:S(2)}, u32[]{:S(2)}) collective-permute-start(bf16[48,768]{1,0:T(8,128)(2,1)S(1)} %collective-permute-done.13), channel_id=1, source_target_pairs={{0,480},{32,0},{64,32},{96,64},{128,96},{160,128},{192,160},{224,1... | collective-permute-start | bytes 221192 | tf_op jit(solution)/shard_map/ppermute | solution.py:22
  101.2 5.0 %collective-permute-start.16 = (bf16[48,768]{1,0:T(8,128)(2,1)S(1)}, bf16[48,768]{1,0:T(8,128)(2,1)S(1)}, u32[]{:S(2)}, u32[]{:S(2)}) collective-permute-start(bf16[48,768]{1,0:T(8,128)(2,1)S(1)} %collective-permute-done.14), channel_id=1, source_target_pairs={{0,32},{32,64},{64,96},{96,128},{128,160},{160,192},{192,224},{224... | collective-permute-start | bytes 221192 | tf_op jit(solution)/shard_map/ppermute | solution.py:19
  122.5 2.7 copy-start.5
  141.2 16.4 %copy-start.4 = (bf16[1,128,1,64]{1,3,2,0:T(8,128)(2,1)S(1)}, bf16[1,128,1,64]{1,3,2,0:T(8,128)(2,1)}, u32[]{:S(2)}) copy-start(bf16[1,128,1,64]{1,3,2,0:T(8,128)(2,1)} %copy.1434) | copy-start | bytes 49156
  141.9 15.1 %copy-start.7 = (bf16[1,16,1,64]{3,2,1,0:T(2,128)(2,1)S(1)}, bf16[1,16,1,64]{3,2,1,0:T(2,128)(2,1)}, u32[]{:S(2)}) copy-start(bf16[1,16,1,64]{3,2,1,0:T(2,128)(2,1)} %get-tuple-element.292) | copy-start | bytes 6148
  142.6 25.2 %copy-start.14 = (pred[512]{0:T(512)(128)(4,1)S(1)}, pred[512]{0:T(512)(128)(4,1)}, u32[]{:S(2)}) copy-start(pred[512]{0:T(512)(128)(4,1)} %copy-done.13) | copy-start | bytes 1540
  142.6 25.2 %copy-start.8 = (f32[3,4,512]{2,1,0:T(4,128)S(1)}, f32[3,4,512]{2,1,0:T(4,128)}, u32[]{:S(2)}) copy-start(f32[3,4,512]{2,1,0:T(4,128)} %custom-call.6) | copy-start | bytes 73732
  142.7 25.2 %copy-start.9 = (f32[3,4,512]{2,1,0:T(4,128)S(1)}, f32[3,4,512]{2,1,0:T(4,128)}, u32[]{:S(2)}) copy-start(f32[3,4,512]{2,1,0:T(4,128)} %custom-call.7) | copy-start | bytes 73732
  153.7 8.7 %collective-permute-start.17 = (bf16[2,12,128,64]{2,3,1,0:T(8,128)(2,1)S(1)}, bf16[2,12,128,64]{2,3,1,0:T(8,128)(2,1)S(1)}, u32[]{:S(2)}, u32[]{:S(2)}) collective-permute-start(bf16[2,12,128,64]{2,3,1,0:T(8,128)(2,1)S(1)} %pad_maximum_fusion.2), channel_id=1, source_target_pairs={{0,1},{1,0},{2,3},{3,2},{4,5},{5,4},{6,7},{7,6},{8,9},{9,8},{10,11... | collective-permute-start | bytes 1179656 | tf_op jit(solution)/shard_map/ppermute | solution.py:53
  163.6 38.3 %collective-permute-start.18 = (bf16[2,12,256,64]{2,3,1,0:T(8,128)(2,1)}, bf16[2,12,256,64]{2,3,1,0:T(8,128)(2,1)}, u32[]{:S(2)}, u32[]{:S(2)}) collective-permute-start(bf16[2,12,256,64]{2,3,1,0:T(8,128)(2,1)} %maximum_select_fusion.1), channel_id=1, source_target_pairs={{0,2},{2,0},{1,3},{3,1},{4,6},{6,4},{5,7},{7,5},{8,10},{10,8},{9,1... | collective-permute-start | bytes 2359304 | tf_op jit(solution)/shard_map/ppermute | solution.py:53
  204.4 1.3 copy-start.11
  204.4 1.3 copy-start.12
  237.3 7.9 %copy-start.6 = (pred[12,512]{1,0:T(8,128)(4,1)S(1)}, pred[12,512]{1,0:T(8,128)(4,1)}, u32[]{:S(2)}) copy-start(pred[12,512]{1,0:T(8,128)(4,1)} %add_compare_fusion) | copy-start | bytes 18436
  249.9 2.5 copy-start
  252.3 0.8 copy-start.1
  252.3 0.8 copy-start.3
  252.4 0.7 copy-start.15
Sparse Core Ops, SparseCore 0:
  9.5 48.2 all-gather.3
  70.0 80.4 all-gather.5
  152.6 41.8 all-gather.7
